TPU v7x, 512 devices: a whole 4x8x8 slice. The times are simulated.
512 devices in a mesh: dp: 64 (over z, y_hi, core), mp: 8 (over y_lo, x).
Axes of the slice: x: 4, y: 8 (y_hi: 4, y_lo: 2; y = y_hi * 2 + y_lo), z: 8, core: 2. Of those that a mesh axis runs over, the one named last changes fastest.
Arguments:
- views: bfloat16 [32768, 256], P('dp'), may hold values from -1 to 1
- partner: int32 [32768], P('dp'), may hold values from 0 to 32767, as said below
- weight: float32 [32768], P('dp'), may hold values from 0.25 to 4
Outputs:
- loss: float32 [32768], P('dp')
- grad: float32 [32768, 256], P('dp')
Inputs may be any that keep to these rules, and one draw needn't show every extreme that they name: partner pairs the views: partner[partner[i]] = i and partner[i] != i.
All inputs are finite; a program needn't handle non-finite values.
Results may differ from a plain program's by a relative error of at most 0.0056.
Values may be sent and summed in bfloat16 or wider, within the bound.
No kernel may reach another device: no remote copies, remote signals or barrier semaphores. Data moves between devices by JAX's collectives and lax.ppermute only.
A program may use at most 64 MiB of HBM per device.

v0:
```python
import jax
import jax.numpy as jnp
from jax import lax
from jax.sharding import Mesh
from jax.sharding import PartitionSpec as P

DP = ("dp_0", "dp_1", "dp_2")
INV_TAU = 10.0
EPS = 1e-06


def sent_to_all(shard, axis):
    count = lax.axis_size(axis)
    return lax.all_to_all(
        jnp.broadcast_to(shard[None], (count, *shard.shape)), axis, 0, 0, tiled=True
    )


def joined_along(parts, dim):
    parts = jnp.moveaxis(parts, 0, dim)
    shape = parts.shape
    return parts.reshape(*shape[:dim], shape[dim] * shape[dim + 1], *shape[dim + 2 :])


def gathered_by_axis(shard, axes, dim):
    far, near = axes
    leading = sent_to_all(shard, far)
    parts = jnp.swapaxes(sent_to_all(leading, near), 0, 1)
    return joined_along(parts.reshape(-1, *shard.shape), dim)


def of_everyone(shard, axis):
    everything = sent_to_all(shard, axis)
    return jnp.sum(everything, axis=0)


def together(arrays, axis):
    vector, at, finished = (jnp.concatenate([a.reshape(-1) for a in arrays]), 0, [])
    subtotal = of_everyone(vector, axis)
    for a in arrays:
        finished.append(subtotal[at : at + a.size].reshape(a.shape))
        at += a.size
    return tuple(finished)


def turned_gather(arrays, axis, dims):
    turned = [jnp.moveaxis(a, dim, 0) for a, dim in zip(arrays, dims)]
    widths = [t[0].size for t in turned]
    both = jnp.concatenate([t.reshape(-1, w) for t, w in zip(turned, widths)], axis=1)
    whole = lax.all_gather(both, axis, axis=0, tiled=True)
    parts = jnp.split(whole, [sum(widths[:k]) for k in range(1, len(widths))], axis=1)
    return tuple(
        (
            jnp.moveaxis(b.reshape(-1, *t.shape[1:]), 0, dim)
            for b, t, dim in zip(parts, turned, dims)
        )
    )


def cut_along(shard, dim, count):
    shape = shard.shape
    parts = shard.reshape(*shape[:dim], count, shape[dim] // count, *shape[dim + 1 :])
    return jnp.moveaxis(parts, dim, 0)


def sent_and_summed(shard, axis, dim):
    parts = cut_along(shard, dim, lax.axis_size(axis))
    arrived = lax.all_to_all(parts, axis, split_axis=0, concat_axis=0, tiled=True)
    return arrived.sum(axis=0)


def gather_directly(shard, axis, dim):
    parts = sent_to_all(shard, axis)
    return joined_along(parts, dim)


def shards(views, partner, weight):
    rows_dev = views.shape[0]
    width = views.shape[1]
    parts = lax.axis_size("mp")
    slot = lax.axis_index("mp")
    block_index = lax.axis_index(DP)
    piece = rows_dev // parts
    floats = views.astype(jnp.float32)
    length = jnp.sqrt(jnp.sum(floats * floats, axis=1) + EPS)
    unit = floats / length[:, None]
    normal = unit.astype(jnp.bfloat16)
    offset = slot * piece
    mine = lax.dynamic_slice_in_dim(normal, offset, piece, 0)
    columns = gathered_by_axis(mine, (("dp_0", "dp_1"), "dp_2"), 0)
    width_cols = columns.shape[0]
    step_cols = min(512, width_cols)
    count = width_cols // step_cols
    position = jnp.arange(width_cols, dtype=jnp.int32)
    col_ids = position // piece * rows_dev + offset + position % piece
    row_ids = block_index * rows_dev + jnp.arange(rows_dev, dtype=jnp.int32)
    id_blocks = col_ids.reshape(count, step_cols)

    def tile(cols_block, ids_block):
        s = (
            lax.dot_general(
                normal, cols_block, (((1,), (1,)), ((), ())), preferred_element_type=jnp.float32
            )
            * INV_TAU
        )
        off = row_ids[:, None] != ids_block[None, :]
        match = partner[:, None] == ids_block[None, :]
        return (s, off, match)

    def forward(carry, inputs):
        cols_block, ids_block = inputs
        s, off, match = tile(cols_block, ids_block)
        total = carry[0] + jnp.sum(jnp.where(off, jnp.exp(s), jnp.float32(0.0)), axis=1)
        positive = carry[1] + jnp.sum(jnp.where(match, s, jnp.float32(0.0)), axis=1)
        return ((total, positive), None)

    zeros_rows = jnp.zeros((rows_dev,), jnp.float32)
    col_blocks = columns.reshape(count, step_cols, width)
    (total, positive), _ = lax.scan(forward, (zeros_rows, zeros_rows), (col_blocks, id_blocks))
    total, positive = together((total, positive), "mp")
    lse = jnp.log(total)
    loss = lse - positive
    lse_mine = lax.dynamic_slice_in_dim(lse, offset, piece, 0)
    weight_mine = lax.dynamic_slice_in_dim(weight, offset, piece, 0)
    col_lse, col_weight = turned_gather((lse_mine, weight_mine), DP, (0, 0))

    def backward(acc, inputs):
        cols_block, ids_block, lse_block, weight_block = inputs
        s, off, match = tile(cols_block, ids_block)
        prow = jnp.exp(s - lse[:, None])
        pcol = jnp.exp(s - lse_block[None, :])
        coef = jnp.where(
            off, weight[:, None] * prow + weight_block[None, :] * pcol, jnp.float32(0.0)
        )
        coef = coef - jnp.where(match, weight[:, None] + weight_block[None, :], jnp.float32(0.0))
        coef = coef.astype(jnp.bfloat16)
        return (acc + jnp.dot(coef, cols_block, preferred_element_type=jnp.float32), None)

    start_acc = jnp.zeros((rows_dev, width), jnp.float32)
    partial_grad, _ = lax.scan(
        backward,
        start_acc,
        (
            col_blocks,
            id_blocks,
            col_lse.reshape(count, step_cols),
            col_weight.reshape(count, step_cols),
        ),
    )
    share = sent_and_summed(partial_grad, "mp", 0) * INV_TAU
    unit_share = lax.dynamic_slice_in_dim(unit, offset, piece, 0)
    length_share = lax.dynamic_slice_in_dim(length, offset, piece, 0)
    finished = (
        share - unit_share * jnp.sum(unit_share * share, axis=1, keepdims=True)
    ) / length_share[:, None]
    grad = gather_directly(finished, "mp", 0)
    return (loss, grad)


def solution(mesh):
    finer = Mesh(mesh.devices.reshape(8, 4, 2, mesh.shape["mp"]), ("dp_0", "dp_1", "dp_2", "mp"))
    placed = (P(DP, None), P(DP), P(DP))
    return jax.shard_map(
        shards, mesh=finer, in_specs=placed, out_specs=(P(DP), P(DP, None)), check_vma=False
    )
```

profile of v0, /device:TPU:1, one launch (start us, length us, event | category | flops | bytes accessed | tf_op | source)
XLA Modules:
  0.0 204.9 jit_solution(12894335910544377624)
XLA Ops:
  0.6 1.1 fusion.31
  1.7 1.1 convert_divide_fusion
  2.9 1.1 broadcast_in_dim.26
  4.0 16.5 %all-to-all-start = ((bf16[32,64,256]{2,1,0:T(8,128)(2,1)}), bf16[32,64,256]{2,1,0:T(8,128)(2,1)S(1)}, u32[]{:S(2)}, u32[]{:S(2)}) async-start(bf16[32,64,256]{2,1,0:T(8,128)(2,1)} %broadcast_in_dim.26), calls=%async_computation | async-start | bytes 2097152 | tf_op jit(solution)/shard_map/all_to_all | solution.py:14
  20.6 31.4 %all-to-all-done = bf16[32,64,256]{2,1,0:T(8,128)(2,1)S(1)} async-done(((bf16[32,64,256]{2,1,0:T(8,128)(2,1)}), bf16[32,64,256]{2,1,0:T(8,128)(2,1)S(1)}, u32[]{:S(2)}, u32[]{:S(2)}) %all-to-all-start) | async-done | bytes 1048608 | tf_op jit(solution)/shard_map/all_to_all | solution.py:14
  51.9 0.2 broadcast_in_dim.27
  52.2 8.1 %all_to_all.26 = bf16[2,32,64,256]{3,2,1,0:T(8,128)(2,1)S(1)} all-to-all(bf16[2,32,64,256]{3,2,1,0:T(8,128)(2,1)S(1)} %broadcast_in_dim.27), channel_id=1, replica_groups=mesh['dp_0'=8,'dp_1'=4,'dp_2'=2,'mp'=8] {'dp_2'}, dimensions={0} | all-to-all | bytes 4194304 | tf_op jit(solution)/shard_map/all_to_all | solution.py:14
  60.3 0.0 copy-start
  60.3 0.1 copy.11
  60.4 0.5 copy-done
  61.0 0.0 copy-start.1
  61.0 4.7 %while.24 = (s32[]{:T(128)}, f32[512]{0:T(512)S(1)}, f32[512]{0:T(512)S(1)}, s32[8,512]{1,0:T(8,128)S(1)}, bf16[8,512,256]{2,1,0:T(8,128)(2,1)S(1)}, /*index=5*/...) while((s32[]{:T(128)}, f32[512]{0:T(512)S(1)}, ...), condition=%wide.region_4.5_spmd.clone, body=%wide.region_1.4_spmd.clone.sunk | while | flops 136054272 | bytes 553083 | solution.py:119
  61.0 0.5 select_reduce_fusion.3
  61.6 0.5 select_reduce_fusion.3
  62.2 0.5 select_reduce_fusion.3
  62.8 0.5 select_reduce_fusion.3
  63.3 0.5 select_reduce_fusion.3
  63.9 0.5 select_reduce_fusion.3
  64.5 0.5 select_reduce_fusion.3
  65.1 0.5 select_reduce_fusion.3
  65.7 0.6 broadcast_in_dim.28
  66.3 4.0 %all-to-all-start.2 = ((f32[8,1,1024]{2,1,0:T(1,128)}), f32[8,1,1024]{2,1,0:T(1,128)S(1)}, u32[]{:S(2)}, u32[]{:S(2)}) async-start(f32[8,1,1024]{2,1,0:T(1,128)} %broadcast_in_dim.28), calls=%async_computation.2 | async-start | bytes 65536 | tf_op jit(solution)/shard_map/all_to_all | solution.py:14
  70.3 0.0 copy-done.1
  70.3 0.1 dynamic-slice_bitcast_fusion
  70.4 5.0 %all-to-all-done.2 = f32[8,1,1024]{2,1,0:T(1,128)S(1)} async-done(((f32[8,1,1024]{2,1,0:T(1,128)}), f32[8,1,1024]{2,1,0:T(1,128)S(1)}, u32[]{:S(2)}, u32[]{:S(2)}) %all-to-all-start.2) | async-done | bytes 32800 | tf_op jit(solution)/shard_map/all_to_all | solution.py:14
  75.5 0.6 slice_log_fusion
  76.0 0.1 dynamic-slice_bitcast_fusion.1
  76.1 80.5 %all-gather = f32[64,64,2]{1,2,0:T(2,128)S(1)} all-gather(f32[1,64,2]{1,2,0:T(2,128)S(1)} %maximum_bitcast_fusion), channel_id=1, replica_groups=mesh['dp_0'=8,'dp_1'=4,'dp_2'=2,'mp'=8] {'dp_0','dp_1','dp_2'}, dimensions={0}, use_global_device_ids=true | all-gather | bytes 33280 | tf_op jit(solution)/shard_map/all_gather | solution.py:50
  156.7 0.1 reshape.51
  156.8 0.1 slice_reduce_fusion
  156.9 22.0 %while.25 = (s32[]{:T(128)}, f32[512,256]{1,0:T(8,128)}, s32[8,512]{1,0:T(8,128)S(1)}, f32[512]{0:T(512)S(1)}, bf16[8,512,256]{2,1,0:T(8,128)(2,1)S(1)}, /*index...) while((s32[]{:T(128)}, f32[512,256]{1,0:T(8,128)}, ...), condition=%wide.region_7.8_spmd.clone, body=%wide.region_6.7_spmd.clone.sunk | while | flops 272105984 | bytes 1868947 | solution.py:140
  156.9 1.8 convolution_add_fusion.2
  158.8 2.8 %convolution_add_fusion.2 = f32[512,256]{1,0:T(8,128)} fusion(bf16[512,256]{1,0:T(8,128)(2,1)S(1)} %get-tuple-element.413, f32[512,256]{1,0:T(8,128)} %get-tuple-element.396, f32[512]{0:T(512)S(1)} %bitcast.61, f32[512]{0:T(512)S(1)} %get-tuple-element.411, s32[512]{0:T(512)S(1)} %get-tuple-element.417, f32[512]{0:T(512)S(1)} %bitcast.60, ...), kind=kOutput, calls=%fused_computation.14.clone.1 | convolution fusion | flops 272105472 | bytes 1854465 | tf_op jit(solution)/shard_map/while/body/eval_jaxpr/dot_general | solution.py:137
  161.7 2.8 %convolution_add_fusion.2 = f32[512,256]{1,0:T(8,128)} fusion(bf16[512,256]{1,0:T(8,128)(2,1)S(1)} %get-tuple-element.413, f32[512,256]{1,0:T(8,128)} %get-tuple-element.396, f32[512]{0:T(512)S(1)} %bitcast.61, f32[512]{0:T(512)S(1)} %get-tuple-element.411, s32[512]{0:T(512)S(1)} %get-tuple-element.417, f32[512]{0:T(512)S(1)} %bitcast.60, ...), kind=kOutput, calls=%fused_computation.14.clone.1 | convolution fusion | flops 272105472 | bytes 1854465 | tf_op jit(solution)/shard_map/while/body/eval_jaxpr/dot_general | solution.py:137
  164.5 2.8 %convolution_add_fusion.2 = f32[512,256]{1,0:T(8,128)} fusion(bf16[512,256]{1,0:T(8,128)(2,1)S(1)} %get-tuple-element.413, f32[512,256]{1,0:T(8,128)} %get-tuple-element.396, f32[512]{0:T(512)S(1)} %bitcast.61, f32[512]{0:T(512)S(1)} %get-tuple-element.411, s32[512]{0:T(512)S(1)} %get-tuple-element.417, f32[512]{0:T(512)S(1)} %bitcast.60, ...), kind=kOutput, calls=%fused_computation.14.clone.1 | convolution fusion | flops 272105472 | bytes 1854465 | tf_op jit(solution)/shard_map/while/body/eval_jaxpr/dot_general | solution.py:137
  167.4 2.8 %convolution_add_fusion.2 = f32[512,256]{1,0:T(8,128)} fusion(bf16[512,256]{1,0:T(8,128)(2,1)S(1)} %get-tuple-element.413, f32[512,256]{1,0:T(8,128)} %get-tuple-element.396, f32[512]{0:T(512)S(1)} %bitcast.61, f32[512]{0:T(512)S(1)} %get-tuple-element.411, s32[512]{0:T(512)S(1)} %get-tuple-element.417, f32[512]{0:T(512)S(1)} %bitcast.60, ...), kind=kOutput, calls=%fused_computation.14.clone.1 | convolution fusion | flops 272105472 | bytes 1854465 | tf_op jit(solution)/shard_map/while/body/eval_jaxpr/dot_general | solution.py:137
  170.3 2.8 %convolution_add_fusion.2 = f32[512,256]{1,0:T(8,128)} fusion(bf16[512,256]{1,0:T(8,128)(2,1)S(1)} %get-tuple-element.413, f32[512,256]{1,0:T(8,128)} %get-tuple-element.396, f32[512]{0:T(512)S(1)} %bitcast.61, f32[512]{0:T(512)S(1)} %get-tuple-element.411, s32[512]{0:T(512)S(1)} %get-tuple-element.417, f32[512]{0:T(512)S(1)} %bitcast.60, ...), kind=kOutput, calls=%fused_computation.14.clone.1 | convolution fusion | flops 272105472 | bytes 1854465 | tf_op jit(solution)/shard_map/while/body/eval_jaxpr/dot_general | solution.py:137
  173.2 2.8 %convolution_add_fusion.2 = f32[512,256]{1,0:T(8,128)} fusion(bf16[512,256]{1,0:T(8,128)(2,1)S(1)} %get-tuple-element.413, f32[512,256]{1,0:T(8,128)} %get-tuple-element.396, f32[512]{0:T(512)S(1)} %bitcast.61, f32[512]{0:T(512)S(1)} %get-tuple-element.411, s32[512]{0:T(512)S(1)} %get-tuple-element.417, f32[512]{0:T(512)S(1)} %bitcast.60, ...), kind=kOutput, calls=%fused_computation.14.clone.1 | convolution fusion | flops 272105472 | bytes 1854465 | tf_op jit(solution)/shard_map/while/body/eval_jaxpr/dot_general | solution.py:137
  176.0 2.8 %convolution_add_fusion.2 = f32[512,256]{1,0:T(8,128)} fusion(bf16[512,256]{1,0:T(8,128)(2,1)S(1)} %get-tuple-element.413, f32[512,256]{1,0:T(8,128)} %get-tuple-element.396, f32[512]{0:T(512)S(1)} %bitcast.61, f32[512]{0:T(512)S(1)} %get-tuple-element.411, s32[512]{0:T(512)S(1)} %get-tuple-element.417, f32[512]{0:T(512)S(1)} %bitcast.60, ...), kind=kOutput, calls=%fused_computation.14.clone.1 | convolution fusion | flops 272105472 | bytes 1854465 | tf_op jit(solution)/shard_map/while/body/eval_jaxpr/dot_general | solution.py:137
  178.9 3.5 %all-to-all-start.3 = ((f32[8,64,256]{2,1,0:T(8,128)}), f32[8,64,256]{2,1,0:T(8,128)S(1)}, u32[]{:S(2)}, u32[]{:S(2)}) async-start(f32[8,64,256]{2,1,0:T(8,128)} %bitcast.6), calls=%async_computation.3 | async-start | bytes 1048576 | tf_op jit(solution)/shard_map/all_to_all | solution.py:68
  182.4 0.1 dynamic_slice.40
  182.4 8.5 %all-to-all-done.3 = f32[8,64,256]{2,1,0:T(8,128)S(1)} async-done(((f32[8,64,256]{2,1,0:T(8,128)}), f32[8,64,256]{2,1,0:T(8,128)S(1)}, u32[]{:S(2)}, u32[]{:S(2)}) %all-to-all-start.3) | async-done | bytes 524320 | tf_op jit(solution)/shard_map/all_to_all | solution.py:68
  191.0 0.1 multiply_reduce_fusion
  191.1 0.1 subtract_divide_fusion
  191.3 12.9 %all_to_all.27 = f32[8,64,256]{2,1,0:T(8,128)S(1)} all-to-all(f32[8,64,256]{2,1,0:T(8,128)S(1)} %broadcast_in_dim.30), channel_id=1, replica_groups=mesh['dp_0'=8,'dp_1'=4,'dp_2'=2,'mp'=8] {'mp'}, dimensions={0} | all-to-all | bytes 1048576 | tf_op jit(solution)/shard_map/all_to_all | solution.py:14
  204.1 0.8 copy.33
  (62 shorter events, 0.6 us)
Async XLA Ops:
  4.0 48.0 %all-to-all-start = ((bf16[32,64,256]{2,1,0:T(8,128)(2,1)}), bf16[32,64,256]{2,1,0:T(8,128)(2,1)S(1)}, u32[]{:S(2)}, u32[]{:S(2)}) async-start(bf16[32,64,256]{2,1,0:T(8,128)(2,1)} %broadcast_in_dim.26), calls=%async_computation | async-start | bytes 2097152 | tf_op jit(solution)/shard_map/all_to_all | solution.py:14
  60.3 0.7 copy-start
  61.0 9.4 %copy-start.1 = (f32[512]{0:T(512)S(1)}, f32[512]{0:T(512)}, u32[]{:S(2)}) copy-start(f32[512]{0:T(512)} %param.9) | copy-start | bytes 6148
  66.3 9.1 %all-to-all-start.2 = ((f32[8,1,1024]{2,1,0:T(1,128)}), f32[8,1,1024]{2,1,0:T(1,128)S(1)}, u32[]{:S(2)}, u32[]{:S(2)}) async-start(f32[8,1,1024]{2,1,0:T(1,128)} %broadcast_in_dim.28), calls=%async_computation.2 | async-start | bytes 65536 | tf_op jit(solution)/shard_map/all_to_all | solution.py:14
  178.9 12.1 %all-to-all-start.3 = ((f32[8,64,256]{2,1,0:T(8,128)}), f32[8,64,256]{2,1,0:T(8,128)S(1)}, u32[]{:S(2)}, u32[]{:S(2)}) async-start(f32[8,64,256]{2,1,0:T(8,128)} %bitcast.6), calls=%async_computation.3 | async-start | bytes 1048576 | tf_op jit(solution)/shard_map/all_to_all | solution.py:68
where the time goes:
time: 206 us; the launch traced here: 205 us
  blocking collectives  101 us (49%)
  waiting for transfers between devices  44.9 us (22%)
  matrix products  25.8 us (13%)
  starting transfers between devices  24 us (12%)
  local copies, waits for them, and re-layouts  4.12 us (2%)
  other arithmetic  3.33 us (2%)
    all_gather x1, blocking collectives, turned_gather(): whole = lax.all_gather(both, axis, axis=0, tiled=True)  80.5 us
    all_to_all x2, waiting for transfers between devices, sent_to_all(): lax.all_to_all(jnp.broadcast_to(shard[None], (count, *shard.shape)), axis...  36.4 us
    dot_general x8, matrix products, backward(): jnp.dot(coef, cols_block, preferred_element_type=jnp.float32)  21.6 us
    all_to_all x2, blocking collectives, sent_to_all(): lax.all_to_all(jnp.broadcast_to(shard[None], (count, *shard.shape)), axis...  21 us
    all_to_all x2, starting transfers between devices, sent_to_all(): lax.all_to_all(jnp.broadcast_to(shard[None], (count, *shard.shape)), axis...  20.5 us
    all_to_all x1, waiting for transfers between devices, sent_and_summed(): lax.all_to_all(parts, axis, split_axis=0, concat_axis=0, tiled=True)  8.51 us
    dot_general x8, matrix products, tile(): lax.dot_general(normal, cols_block, (((1,), (1,)), ((), ())), preferred_e...  4.18 us
  transfers between devices with their start and end apart: 3, of which 3 were waited for; matrix products, arithmetic and copies ran while one was open for 0% of the time, Pallas kernels for 0%

commit v1 on v0

--- a/solution.py
+++ b/solution.py
@@ -47,7 +47,10 @@
     turned = [jnp.moveaxis(a, dim, 0) for a, dim in zip(arrays, dims)]
     widths = [t[0].size for t in turned]
     both = jnp.concatenate([t.reshape(-1, w) for t, w in zip(turned, widths)], axis=1)
-    whole = lax.all_gather(both, axis, axis=0, tiled=True)
+    devices = lax.axis_size(axis)
+    pieces = jnp.stack([both for _ in range(devices)])
+    pieces = lax.all_to_all(pieces, axis, split_axis=0, concat_axis=0)
+    whole = jnp.concatenate(pieces, axis=0)
     parts = jnp.split(whole, [sum(widths[:k]) for k in range(1, len(widths))], axis=1)
     return tuple(
         (

time: 206 us -> 147 us (0.71)
  blocking collectives: 101 us -> 21.3 us
  waiting for transfers between devices: 44.9 us -> 56.3 us
  starting transfers between devices: 24 us -> 32.1 us
    all_gather x1 -> x0, blocking collectives: 80.5 us -> none  [turned_gather(): whole = lax.all_gather(both, axis, axis=0, tiled=True)]
    all_to_all x0 -> x1, waiting for transfers between devices: none -> 11.8 us  [turned_gather(): pieces = lax.all_to_all(pieces, axis, split_axis=0, concat_axis=0)]
    all_to_all x0 -> x1, starting transfers between devices: none -> 8.05 us  [turned_gather(): pieces = lax.all_to_all(pieces, axis, split_axis=0, concat_axis=0)]
  transfers between devices with their start and end apart: 3 -> 4, of which waited for: 3 -> 4; matrix products, arithmetic and copies ran while one was open for 0% -> 0% of each run, Pallas kernels for 0% -> 0%
where the time goes in v1:
time: 147 us; the launch traced here: 146 us
  waiting for transfers between devices  56.3 us (38%)
  starting transfers between devices  32.1 us (22%)
  matrix products  25.7 us (17%)
  blocking collectives  21.3 us (14%)
  local copies, waits for them, and re-layouts  5.56 us (4%)
  other arithmetic  4.09 us (3%)
    all_to_all x2, waiting for transfers between devices, sent_to_all(): lax.all_to_all(jnp.broadcast_to(shard[None], (count, *shard.shape)), axis...  36.4 us
    dot_general x8, matrix products, backward(): jnp.dot(coef, cols_block, preferred_element_type=jnp.float32)  21.6 us
    all_to_all x2, blocking collectives, sent_to_all(): lax.all_to_all(jnp.broadcast_to(shard[None], (count, *shard.shape)), axis...  21.3 us
    all_to_all x2, starting transfers between devices, sent_to_all(): lax.all_to_all(jnp.broadcast_to(shard[None], (count, *shard.shape)), axis...  20.5 us
    all_to_all x1, waiting for transfers between devices, turned_gather(): pieces = lax.all_to_all(pieces, axis, split_axis=0, concat_axis=0)  11.8 us
    all_to_all x1, waiting for transfers between devices, sent_and_summed(): lax.all_to_all(parts, axis, split_axis=0, concat_axis=0, tiled=True)  8.07 us
    all_to_all x1, starting transfers between devices, turned_gather(): pieces = lax.all_to_all(pieces, axis, split_axis=0, concat_axis=0)  8.05 us
    dot_general x8, matrix products, tile(): lax.dot_general(normal, cols_block, (((1,), (1,)), ((), ())), preferred_e...  4.18 us
  transfers between devices with their start and end apart: 4, of which 4 were waited for; matrix products, arithmetic and copies ran while one was open for 0% of the time, Pallas kernels for 0%

profile of v1, /device:TPU:1, one launch (start us, length us, event | category | flops | bytes accessed | tf_op | source)
XLA Modules:
  0.0 146.4 jit_solution(4092966686326012875)
XLA Ops:
  0.6 1.1 fusion.31
  1.7 1.1 convert_divide_fusion
  2.9 1.1 broadcast_in_dim.26
  4.0 16.5 %all-to-all-start = ((bf16[32,64,256]{2,1,0:T(8,128)(2,1)}), bf16[32,64,256]{2,1,0:T(8,128)(2,1)S(1)}, u32[]{:S(2)}, u32[]{:S(2)}) async-start(bf16[32,64,256]{2,1,0:T(8,128)(2,1)} %broadcast_in_dim.26), calls=%async_computation | async-start | bytes 2097152 | tf_op jit(solution)/shard_map/all_to_all | solution.py:14
  20.5 31.4 %all-to-all-done = bf16[32,64,256]{2,1,0:T(8,128)(2,1)S(1)} async-done(((bf16[32,64,256]{2,1,0:T(8,128)(2,1)}), bf16[32,64,256]{2,1,0:T(8,128)(2,1)S(1)}, u32[]{:S(2)}, u32[]{:S(2)}) %all-to-all-start) | async-done | bytes 1048608 | tf_op jit(solution)/shard_map/all_to_all | solution.py:14
  51.9 0.2 broadcast_in_dim.27
  52.2 8.1 %all_to_all.31 = bf16[2,32,64,256]{3,2,1,0:T(8,128)(2,1)S(1)} all-to-all(bf16[2,32,64,256]{3,2,1,0:T(8,128)(2,1)S(1)} %broadcast_in_dim.27), channel_id=1, replica_groups=mesh['dp_0'=8,'dp_1'=4,'dp_2'=2,'mp'=8] {'dp_2'}, dimensions={0} | all-to-all | bytes 4194304 | tf_op jit(solution)/shard_map/all_to_all | solution.py:14
  60.3 0.1 copy.9
  60.4 0.5 copy-done
  61.0 4.7 %while.24 = (s32[]{:T(128)}, f32[512]{0:T(512)S(1)}, f32[512]{0:T(512)S(1)}, s32[8,512]{1,0:T(8,128)S(1)}, bf16[8,512,256]{2,1,0:T(8,128)(2,1)S(1)}, /*index=5*/...) while((s32[]{:T(128)}, f32[512]{0:T(512)S(1)}, ...), condition=%wide.region_4.5_spmd.clone, body=%wide.region_1.4_spmd.clone.sunk | while | flops 136054272 | bytes 553083 | solution.py:122
  61.0 0.5 select_reduce_fusion.3
  61.6 0.5 select_reduce_fusion.3
  62.2 0.5 select_reduce_fusion.3
  62.8 0.5 select_reduce_fusion.3
  63.3 0.5 select_reduce_fusion.3
  63.9 0.5 select_reduce_fusion.3
  64.5 0.5 select_reduce_fusion.3
  65.1 0.5 select_reduce_fusion.3
  65.7 0.6 broadcast_in_dim.28
  66.3 4.0 %all-to-all-start.2 = ((f32[8,1,1024]{2,1,0:T(1,128)}), f32[8,1,1024]{2,1,0:T(1,128)S(1)}, u32[]{:S(2)}, u32[]{:S(2)}) async-start(f32[8,1,1024]{2,1,0:T(1,128)} %broadcast_in_dim.28), calls=%async_computation.2 | async-start | bytes 65536 | tf_op jit(solution)/shard_map/all_to_all | solution.py:14
  70.3 0.1 dynamic-slice_bitcast_fusion
  70.4 5.0 %all-to-all-done.2 = f32[8,1,1024]{2,1,0:T(1,128)S(1)} async-done(((f32[8,1,1024]{2,1,0:T(1,128)}), f32[8,1,1024]{2,1,0:T(1,128)S(1)}, u32[]{:S(2)}, u32[]{:S(2)}) %all-to-all-start.2) | async-done | bytes 32800 | tf_op jit(solution)/shard_map/all_to_all | solution.py:14
  75.5 0.6 slice_log_fusion
  76.1 0.1 dynamic-slice_bitcast_fusion.1
  76.2 0.7 reshape.68
  76.9 8.0 %all-to-all-start.3 = ((f32[64,1,128]{2,1,0:T(1,128)}), f32[64,1,128]{2,1,0:T(1,128)S(1)}, u32[]{:S(2)}, u32[]{:S(2)}) async-start(f32[64,1,128]{2,1,0:T(1,128)} %reshape.68), calls=%async_computation.3 | async-start | bytes 65536 | tf_op jit(solution)/shard_map/all_to_all | solution.py:52
  85.0 11.8 %all-to-all-done.3 = f32[64,1,128]{2,1,0:T(1,128)S(1)} async-done(((f32[64,1,128]{2,1,0:T(1,128)}), f32[64,1,128]{2,1,0:T(1,128)S(1)}, u32[]{:S(2)}, u32[]{:S(2)}) %all-to-all-start.3) | async-done | bytes 32800 | tf_op jit(solution)/shard_map/all_to_all | solution.py:52
  96.7 0.6 broadcast.107
  97.3 0.8 reduce.9
  98.1 0.1 reshape.69
  98.2 0.1 reshape.53
  98.3 0.1 slice_reduce_fusion
  98.4 22.0 %while.25 = (s32[]{:T(128)}, f32[512,256]{1,0:T(8,128)}, s32[8,512]{1,0:T(8,128)S(1)}, f32[512]{0:T(512)S(1)}, bf16[8,512,256]{2,1,0:T(8,128)(2,1)S(1)}, /*index...) while((s32[]{:T(128)}, f32[512,256]{1,0:T(8,128)}, ...), condition=%wide.region_7.8_spmd.clone, body=%wide.region_6.7_spmd.clone.sunk | while | flops 272105984 | bytes 1868947 | solution.py:143
  98.5 1.8 %convolution_add_fusion.2 = f32[512,256]{1,0:T(8,128)} fusion(bf16[512,256]{1,0:T(8,128)(2,1)S(1)} %get-tuple-element.413, f32[512,256]{1,0:T(8,128)} %get-tuple-element.396, f32[512]{0:T(512)S(1)} %bitcast.63, f32[512]{0:T(512)S(1)} %get-tuple-element.411, s32[512]{0:T(512)S(1)} %get-tuple-element.417, f32[512]{0:T(512)S(1)} %bitcast.62, ...), kind=kOutput, calls=%fused_computation.14.clone.1 | convolution fusion | flops 272105472 | bytes 1854465 | tf_op jit(solution)/shard_map/while/body/eval_jaxpr/dot_general | solution.py:140
  100.3 2.8 %convolution_add_fusion.2 = f32[512,256]{1,0:T(8,128)} fusion(bf16[512,256]{1,0:T(8,128)(2,1)S(1)} %get-tuple-element.413, f32[512,256]{1,0:T(8,128)} %get-tuple-element.396, f32[512]{0:T(512)S(1)} %bitcast.63, f32[512]{0:T(512)S(1)} %get-tuple-element.411, s32[512]{0:T(512)S(1)} %get-tuple-element.417, f32[512]{0:T(512)S(1)} %bitcast.62, ...), kind=kOutput, calls=%fused_computation.14.clone.1 | convolution fusion | flops 272105472 | bytes 1854465 | tf_op jit(solution)/shard_map/while/body/eval_jaxpr/dot_general | solution.py:140
  103.2 2.8 %convolution_add_fusion.2 = f32[512,256]{1,0:T(8,128)} fusion(bf16[512,256]{1,0:T(8,128)(2,1)S(1)} %get-tuple-element.413, f32[512,256]{1,0:T(8,128)} %get-tuple-element.396, f32[512]{0:T(512)S(1)} %bitcast.63, f32[512]{0:T(512)S(1)} %get-tuple-element.411, s32[512]{0:T(512)S(1)} %get-tuple-element.417, f32[512]{0:T(512)S(1)} %bitcast.62, ...), kind=kOutput, calls=%fused_computation.14.clone.1 | convolution fusion | flops 272105472 | bytes 1854465 | tf_op jit(solution)/shard_map/while/body/eval_jaxpr/dot_general | solution.py:140
  106.1 2.8 %convolution_add_fusion.2 = f32[512,256]{1,0:T(8,128)} fusion(bf16[512,256]{1,0:T(8,128)(2,1)S(1)} %get-tuple-element.413, f32[512,256]{1,0:T(8,128)} %get-tuple-element.396, f32[512]{0:T(512)S(1)} %bitcast.63, f32[512]{0:T(512)S(1)} %get-tuple-element.411, s32[512]{0:T(512)S(1)} %get-tuple-element.417, f32[512]{0:T(512)S(1)} %bitcast.62, ...), kind=kOutput, calls=%fused_computation.14.clone.1 | convolution fusion | flops 272105472 | bytes 1854465 | tf_op jit(solution)/shard_map/while/body/eval_jaxpr/dot_general | solution.py:140
  109.0 2.8 %convolution_add_fusion.2 = f32[512,256]{1,0:T(8,128)} fusion(bf16[512,256]{1,0:T(8,128)(2,1)S(1)} %get-tuple-element.413, f32[512,256]{1,0:T(8,128)} %get-tuple-element.396, f32[512]{0:T(512)S(1)} %bitcast.63, f32[512]{0:T(512)S(1)} %get-tuple-element.411, s32[512]{0:T(512)S(1)} %get-tuple-element.417, f32[512]{0:T(512)S(1)} %bitcast.62, ...), kind=kOutput, calls=%fused_computation.14.clone.1 | convolution fusion | flops 272105472 | bytes 1854465 | tf_op jit(solution)/shard_map/while/body/eval_jaxpr/dot_general | solution.py:140
  111.8 2.8 %convolution_add_fusion.2 = f32[512,256]{1,0:T(8,128)} fusion(bf16[512,256]{1,0:T(8,128)(2,1)S(1)} %get-tuple-element.413, f32[512,256]{1,0:T(8,128)} %get-tuple-element.396, f32[512]{0:T(512)S(1)} %bitcast.63, f32[512]{0:T(512)S(1)} %get-tuple-element.411, s32[512]{0:T(512)S(1)} %get-tuple-element.417, f32[512]{0:T(512)S(1)} %bitcast.62, ...), kind=kOutput, calls=%fused_computation.14.clone.1 | convolution fusion | flops 272105472 | bytes 1854465 | tf_op jit(solution)/shard_map/while/body/eval_jaxpr/dot_general | solution.py:140
  114.7 2.8 %convolution_add_fusion.2 = f32[512,256]{1,0:T(8,128)} fusion(bf16[512,256]{1,0:T(8,128)(2,1)S(1)} %get-tuple-element.413, f32[512,256]{1,0:T(8,128)} %get-tuple-element.396, f32[512]{0:T(512)S(1)} %bitcast.63, f32[512]{0:T(512)S(1)} %get-tuple-element.411, s32[512]{0:T(512)S(1)} %get-tuple-element.417, f32[512]{0:T(512)S(1)} %bitcast.62, ...), kind=kOutput, calls=%fused_computation.14.clone.1 | convolution fusion | flops 272105472 | bytes 1854465 | tf_op jit(solution)/shard_map/while/body/eval_jaxpr/dot_general | solution.py:140
  117.6 2.8 %convolution_add_fusion.2 = f32[512,256]{1,0:T(8,128)} fusion(bf16[512,256]{1,0:T(8,128)(2,1)S(1)} %get-tuple-element.413, f32[512,256]{1,0:T(8,128)} %get-tuple-element.396, f32[512]{0:T(512)S(1)} %bitcast.63, f32[512]{0:T(512)S(1)} %get-tuple-element.411, s32[512]{0:T(512)S(1)} %get-tuple-element.417, f32[512]{0:T(512)S(1)} %bitcast.62, ...), kind=kOutput, calls=%fused_computation.14.clone.1 | convolution fusion | flops 272105472 | bytes 1854465 | tf_op jit(solution)/shard_map/while/body/eval_jaxpr/dot_general | solution.py:140
  120.4 3.5 %all-to-all-start.4 = ((f32[8,64,256]{2,1,0:T(8,128)}), f32[8,64,256]{2,1,0:T(8,128)S(1)}, u32[]{:S(2)}, u32[]{:S(2)}) async-start(f32[8,64,256]{2,1,0:T(8,128)} %bitcast.5), calls=%async_computation.4 | async-start | bytes 1048576 | tf_op jit(solution)/shard_map/all_to_all | solution.py:71
  123.9 0.1 dynamic_slice.40
  124.0 8.1 %all-to-all-done.4 = f32[8,64,256]{2,1,0:T(8,128)S(1)} async-done(((f32[8,64,256]{2,1,0:T(8,128)}), f32[8,64,256]{2,1,0:T(8,128)S(1)}, u32[]{:S(2)}, u32[]{:S(2)}) %all-to-all-start.4) | async-done | bytes 524320 | tf_op jit(solution)/shard_map/all_to_all | solution.py:71
  132.1 0.1 multiply_reduce_fusion
  132.2 0.1 subtract_divide_fusion
  132.4 13.2 %all_to_all.32 = f32[8,64,256]{2,1,0:T(8,128)S(1)} all-to-all(f32[8,64,256]{2,1,0:T(8,128)S(1)} %broadcast_in_dim.30), channel_id=1, replica_groups=mesh['dp_0'=8,'dp_1'=4,'dp_2'=2,'mp'=8] {'mp'}, dimensions={0} | all-to-all | bytes 1048576 | tf_op jit(solution)/shard_map/all_to_all | solution.py:14
  145.6 0.8 copy.31
  (66 shorter events, 0.6 us)
Async XLA Ops:
  4.0 48.0 %all-to-all-start = ((bf16[32,64,256]{2,1,0:T(8,128)(2,1)}), bf16[32,64,256]{2,1,0:T(8,128)(2,1)S(1)}, u32[]{:S(2)}, u32[]{:S(2)}) async-start(bf16[32,64,256]{2,1,0:T(8,128)(2,1)} %broadcast_in_dim.26), calls=%async_computation | async-start | bytes 2097152 | tf_op jit(solution)/shard_map/all_to_all | solution.py:14
  60.3 0.7 copy-start
  61.0 9.4 %copy-start.1 = (f32[512]{0:T(512)S(1)}, f32[512]{0:T(512)}, u32[]{:S(2)}) copy-start(f32[512]{0:T(512)} %param.9) | copy-start | bytes 6148
  66.3 9.1 %all-to-all-start.2 = ((f32[8,1,1024]{2,1,0:T(1,128)}), f32[8,1,1024]{2,1,0:T(1,128)S(1)}, u32[]{:S(2)}, u32[]{:S(2)}) async-start(f32[8,1,1024]{2,1,0:T(1,128)} %broadcast_in_dim.28), calls=%async_computation.2 | async-start | bytes 65536 | tf_op jit(solution)/shard_map/all_to_all | solution.py:14
  76.9 19.9 %all-to-all-start.3 = ((f32[64,1,128]{2,1,0:T(1,128)}), f32[64,1,128]{2,1,0:T(1,128)S(1)}, u32[]{:S(2)}, u32[]{:S(2)}) async-start(f32[64,1,128]{2,1,0:T(1,128)} %reshape.68), calls=%async_computation.3 | async-start | bytes 65536 | tf_op jit(solution)/shard_map/all_to_all | solution.py:52
  120.4 11.7 %all-to-all-start.4 = ((f32[8,64,256]{2,1,0:T(8,128)}), f32[8,64,256]{2,1,0:T(8,128)S(1)}, u32[]{:S(2)}, u32[]{:S(2)}) async-start(f32[8,64,256]{2,1,0:T(8,128)} %bitcast.5), calls=%async_computation.4 | async-start | bytes 1048576 | tf_op jit(solution)/shard_map/all_to_all | solution.py:71
